TPU v7x, 256 devices: a whole 4x4x8 slice. The times are simulated.
256 devices in a mesh: space: 8 (over x, core), mem: 32 (over z, y).
Axes of the slice: x: 4, y: 4, z: 8, core: 2. Of those that a mesh axis runs over, the one named last changes fastest.
Arguments:
- prior_ensemble: float32 [512, 65536], P('mem', 'space'), may hold values from -5 to 5
- terminal_particles: float32 [512, 65536], P(None, ('space', 'mem')), may hold values from -5 to 5
- reverse_perturbation: float32 [3, 512, 65536], P(None, None, ('space', 'mem')), may hold values from -6 to 6
- measured_angles: float32 [65536], P(('space', 'mem')), may hold values from -1.3 to 1.3
Outputs:
- analysis: float32 [512, 65536], P(None, ('space', 'mem'))
All inputs are finite; a program needn't handle non-finite values.
Results may differ from a plain program's by a relative error of at most 0.0003.
Values sent between devices are 32-bit elements; how exact they have to be, the bound alone decides.
No kernel may reach another device: no remote copies, remote signals or barrier semaphores. Data moves between devices by JAX's collectives and lax.ppermute only.
A program may use at most 64 MiB of HBM per device.

v0:
```python
import math
import jax
import jax.numpy as jnp
from jax import lax
from jax.sharding import PartitionSpec as P

ITERS = 3


def member_weights(inner_pairing_matrix, particle_lengths, alpha, sigma2, temper):
    logits = (2.0 * alpha * inner_pairing_matrix - alpha * alpha * particle_lengths[None, :]) / (
        2.0 * sigma2 * temper
    )
    return jax.nn.softmax(logits, axis=1)


def per_device(prior_ensemble, terminal_particles, reverse_perturbation, measured_angles):
    peak_log_likelihood = lax.Precision.HIGHEST
    particle_vectors = lax.all_to_all(
        prior_ensemble, "mem", split_axis=1, concat_axis=0, tiled=True
    )
    devices_all = lax.axis_size("space") * lax.axis_size("mem")
    temper = math.sqrt(particle_vectors.shape[1] * devices_all)
    particle_lengths = lax.psum(
        jnp.sum(particle_vectors * particle_vectors, axis=1), ("space", "mem")
    )
    gaussian_variates = terminal_particles
    for step in range(ITERS):
        t = 1.0 - step / ITERS
        dt = 1.0 / ITERS
        alpha = 1.0 - 0.5 * t
        drift = -0.5 / alpha
        g2 = 1.0 + t / alpha
        damp = 1.0 - t
        partial_gram = jnp.einsum(
            "sv,mv->sm",
            gaussian_variates,
            particle_vectors,
            precision=peak_log_likelihood,
            preferred_element_type=jnp.float32,
        )
        inner_pairing_matrix = lax.psum(partial_gram, ("space", "mem"))
        annealed_importance = member_weights(
            inner_pairing_matrix, particle_lengths, alpha, t, temper
        )
        mixed_correction = jnp.dot(
            annealed_importance,
            particle_vectors,
            precision=peak_log_likelihood,
            preferred_element_type=jnp.float32,
        )
        score = -(gaussian_variates - alpha * mixed_correction) / t + damp * 4.0 * (
            measured_angles[None, :] - jnp.arctan(gaussian_variates)
        ) / (1.0 + gaussian_variates * gaussian_variates)
        gaussian_variates = (
            gaussian_variates
            + dt * (-drift * gaussian_variates + g2 * score)
            + math.sqrt(dt * g2) * reverse_perturbation[step]
        )
    return gaussian_variates


def solution(mesh):
    in_specs = (
        P("mem", "space"),
        P(None, ("space", "mem")),
        P(None, None, ("space", "mem")),
        P(("space", "mem")),
    )
    out_specs = P(None, ("space", "mem"))
    return jax.shard_map(
        per_device, mesh=mesh, in_specs=in_specs, out_specs=out_specs, check_vma=False
    )
```

profile of v0, /device:TPU:2, one launch (start us, length us, event | category | flops | bytes accessed | tf_op | source)
XLA Modules:
  0.0 836.8 jit_solution(16117803827665191883)
XLA Ops:
  6.5 0.0 copy-start.3
  6.5 0.0 all-reduce.4.cloned.1.call-start
  6.5 1.2 copy.9
  7.7 29.0 %all_to_all.19 = f32[16,32,256]{2,0,1:T(8,128)S(1)} all-to-all(f32[16,32,256]{2,0,1:T(8,128)S(1)} %bitcast.30), channel_id=1, replica_groups=mesh['space'=8,'mem'=32] {'mem'}, dimensions={1} | all-to-all | bytes 1048576 | tf_op jit(solution)/shard_map/all_to_all | solution.py:19
  36.7 0.0 copy-start
  36.7 0.0 copy-done.3
  36.7 2.1 fusion.2
  38.8 0.0 all-reduce.4.cloned.1.call-update
  38.8 0.0 all-reduce.6.cloned.1.call-start
  38.8 0.0 copy-done
  38.8 0.1 fusion
  39.0 0.1 reduce_sum.39
  39.1 72.9 %psum.29 = f32[512]{0:T(512)S(1)} all-reduce(f32[512]{0:T(512)S(1)} %reduce_sum.39), channel_id=1, replica_groups=mesh['space'=8,'mem'=32] {'space','mem'}, use_global_device_ids=true, to_apply=%region_2.0 | all-reduce | flops 512 | bytes 4096 | tf_op jit(solution)/shard_map/psum | solution.py:24
  112.0 179.0 %all-reduce.4.cloned.1.call-done = f32[512,512]{1,0:T(8,128)} async-done(((f32[512,512]{1,0:T(8,128)}), f32[512,512]{1,0:T(8,128)}) %all-reduce.4.cloned.1.call-update) | async-done | bytes 1048592 | tf_op jit(solution)/shard_map/psum | solution.py:42
  291.0 0.0 copy-start.6
  291.0 2.4 subtract_multiply_fusion.2
  293.4 0.0 copy-start.1
  293.4 0.0 copy-start.5
  293.4 3.7 online-softmax
  297.1 0.0 copy-done.6
  297.1 0.0 copy-done.1
  297.1 0.0 copy-done.5
  297.1 3.9 fusion.1
  301.1 0.0 all-reduce.6.cloned.1.call-update
  301.1 0.2 all-reduce.8.cloned.1.call-start
  301.3 254.5 %all-reduce.6.cloned.1.call-done = f32[512,512]{1,0:T(8,128)} async-done(((f32[512,512]{1,0:T(8,128)}), f32[512,512]{1,0:T(8,128)}) %all-reduce.6.cloned.1.call-update) | async-done | bytes 1048592 | tf_op jit(solution)/shard_map/psum | solution.py:42
  555.8 2.4 subtract_multiply_fusion.1
  558.2 0.0 copy-start.4
  558.2 3.6 online-softmax.1
  561.8 0.0 copy-done.4
  561.8 0.0 copy-start.2
  561.8 2.8 bitcast_add_fusion.1
  564.6 0.0 copy-done.2
  564.6 2.1 fusion.3
  566.7 0.0 all-reduce.8.cloned.1.call-update
  566.7 254.9 %all-reduce.8.cloned.1.call-done = f32[512,512]{1,0:T(8,128)} async-done(((f32[512,512]{1,0:T(8,128)}), f32[512,512]{1,0:T(8,128)}) %all-reduce.8.cloned.1.call-update) | async-done | bytes 1048592 | tf_op jit(solution)/shard_map/psum | solution.py:42
  821.6 2.4 subtract_multiply_fusion
  824.0 3.6 online-softmax.2
  827.6 2.7 bitcast_add_fusion
  (1 shorter events, 0.0 us)
Async XLA Ops:
  6.5 30.2 %copy-start.3 = (f32[512,256]{1,0:T(8,128)S(1)}, f32[512,256]{1,0:T(8,128)}, u32[]{:S(2)}) copy-start(f32[512,256]{1,0:T(8,128)} %param.5) | copy-start | bytes 1572868
  6.5 284.5 %all-reduce.4.cloned.1.call-start = ((), (), s32[]{:S(2)}) async-start(), calls=%async_computation.1 | async-start | bytes 2097152 | tf_op jit(solution)/shard_map/psum | solution.py:42
  36.7 2.1 copy-start
  38.8 517.0 %all-reduce.6.cloned.1.call-start = ((), (), s32[]{:S(2)}) async-start(), calls=%async_computation.2 | async-start | bytes 2097152 | tf_op jit(solution)/shard_map/psum | solution.py:42
  291.0 6.1 copy-start.6
  293.4 3.7 copy-start.1
  293.4 3.7 copy-start.5
  301.1 520.5 %all-reduce.8.cloned.1.call-start = ((), (), s32[]{:S(2)}) async-start(), calls=%async_computation.3 | async-start | bytes 2097152 | tf_op jit(solution)/shard_map/psum | solution.py:42
  558.2 3.6 copy-start.4
  561.8 2.8 copy-start.2
Sparse Core Ops, SparseCore 0:
  38.9 252.0 all-reduce.3
  301.2 254.5 all-reduce.5
  566.8 254.7 all-reduce.7
where the time goes:
time: 837 us
  waiting for transfers between devices  688 us (82%)
  blocking collectives  102 us (12%)
  between operations  13.1 us (2%)
  other arithmetic  12.8 us (2%)
  Pallas kernels  10.9 us (1%)
    psum x3, waiting for transfers between devices, per_device(): inner_pairing_matrix = lax.psum(partial_gram, ('space', 'mem'))  688 us
    psum x1, blocking collectives, per_device(): lax.psum(jnp.sum(particle_vectors * particle_vectors, axis=1), ('space',...  72.9 us
    all_to_all x1, blocking collectives, per_device(): lax.all_to_all(prior_ensemble, 'mem', split_axis=1, concat_axis=0, tiled=...  29 us
  transfers between devices with their start and end apart: 3, of which 3 were waited for; matrix products, arithmetic and copies ran while one was open for 0% of the time, Pallas kernels for 0%

commit v1 on v0

--- a/solution.py
+++ b/solution.py
@@ -39,7 +39,9 @@
             precision=peak_log_likelihood,
             preferred_element_type=jnp.float32,
         )
-        inner_pairing_matrix = lax.psum(partial_gram, ("space", "mem"))
+        inner_pairing_matrix = partial_gram
+        for axis in ("mem", "space"):
+            inner_pairing_matrix = lax.psum(inner_pairing_matrix, axis)
         annealed_importance = member_weights(
             inner_pairing_matrix, particle_lengths, alpha, t, temper
         )

time: 837 us -> 725 us (0.87)
  waiting for transfers between devices: 688 us -> 573 us
    psum x3 -> x6, waiting for transfers between devices: 688 us -> 573 us  [per_device(): inner_pairing_matrix = lax.psum(inner_pairing_matrix, axis)]
  transfers between devices with their start and end apart: 3 -> 6, of which waited for: 3 -> 5; matrix products, arithmetic and copies ran while one was open for 0% -> 0% of each run, Pallas kernels for 0% -> 0%
where the time goes in v1:
time: 725 us; the launch traced here: 722 us
  waiting for transfers between devices  573 us (79%)
  blocking collectives  102 us (14%)
  between operations  13.5 us (2%)
  other arithmetic  12.7 us (2%)
  Pallas kernels  10.9 us (2%)
  matrix products  8.04 us (1%)
    psum x6, waiting for transfers between devices, per_device(): inner_pairing_matrix = lax.psum(inner_pairing_matrix, axis)  573 us
    psum x1, blocking collectives, per_device(): lax.psum(jnp.sum(particle_vectors * particle_vectors, axis=1), ('space',...  73 us
    all_to_all x1, blocking collectives, per_device(): lax.all_to_all(prior_ensemble, 'mem', split_axis=1, concat_axis=0, tiled=...  29 us
  transfers between devices with their start and end apart: 6, of which 5 were waited for; matrix products, arithmetic and copies ran while one was open for 0% of the time, Pallas kernels for 0%

profile of v1, /device:TPU:2, one launch (start us, length us, event | category | flops | bytes accessed | tf_op | source)
XLA Modules:
  0.0 721.9 jit_solution(6922162133194333580)
XLA Ops:
  6.5 0.0 copy-start.3
  6.5 0.0 all-reduce.7.cloned.1.call-start
  6.5 1.2 copy.9
  7.7 29.0 %all_to_all.19 = f32[16,32,256]{2,0,1:T(8,128)S(1)} all-to-all(f32[16,32,256]{2,0,1:T(8,128)S(1)} %bitcast.30), channel_id=1, replica_groups=mesh['space'=8,'mem'=32] {'mem'}, dimensions={1} | all-to-all | bytes 1048576 | tf_op jit(solution)/shard_map/all_to_all | solution.py:19
  36.7 0.0 copy-start
  36.7 0.0 copy-done.3
  36.7 2.1 fusion.2
  38.8 0.0 all-reduce.7.cloned.1.call-update
  38.8 0.0 all-reduce.9.cloned.1.call-start
  38.8 145.9 %all-reduce.7.cloned.1.call-done = f32[512,512]{1,0:T(8,128)} async-done(((f32[512,512]{1,0:T(8,128)}), f32[512,512]{1,0:T(8,128)}) %all-reduce.7.cloned.1.call-update) | async-done | bytes 1048592 | tf_op jit(solution)/shard_map/psum | solution.py:44
  184.7 0.0 all-reduce.9.cloned.1.call-update
  184.7 0.0 all-reduce.11.cloned.1.call-start
  184.8 0.0 copy-done
  184.8 0.1 fusion
  184.9 0.1 reduce_sum.39
  185.0 73.0 %psum.51 = f32[512]{0:T(512)S(1)} all-reduce(f32[512]{0:T(512)S(1)} %reduce_sum.39), channel_id=1, replica_groups=mesh['space'=8,'mem'=32] {'space','mem'}, use_global_device_ids=true, to_apply=%region_3.0 | all-reduce | flops 512 | bytes 4096 | tf_op jit(solution)/shard_map/psum | solution.py:24
  258.0 0.0 all-reduce.9.cloned.1.call-done
  258.0 0.0 copy-start.6
  258.0 2.3 subtract_multiply_fusion.2
  260.3 0.0 copy-start.1
  260.3 0.0 copy-start.5
  260.3 3.7 online-softmax
  264.0 0.0 copy-done.6
  264.0 0.0 copy-done.1
  264.0 0.0 copy-done.5
  264.1 3.9 fusion.1
  268.0 0.0 all-reduce.11.cloned.1.call-update
  268.0 0.0 all-reduce.13.cloned.1.call-start
  268.0 146.6 %all-reduce.11.cloned.1.call-done = f32[512,512]{1,0:T(8,128)} async-done(((f32[512,512]{1,0:T(8,128)}), f32[512,512]{1,0:T(8,128)}) %all-reduce.11.cloned.1.call-update) | async-done | bytes 1048592 | tf_op jit(solution)/shard_map/psum | solution.py:44
  414.6 0.0 all-reduce.13.cloned.1.call-update
  414.7 0.0 all-reduce.15.cloned.1.call-start
  414.7 64.7 %all-reduce.13.cloned.1.call-done = f32[512,512]{1,0:T(8,128)} async-done(((f32[512,512]{1,0:T(8,128)}), f32[512,512]{1,0:T(8,128)}) %all-reduce.13.cloned.1.call-update) | async-done | bytes 1048592 | tf_op jit(solution)/shard_map/psum | solution.py:44
  479.5 2.3 subtract_multiply_fusion.1
  481.8 0.0 copy-start.4
  481.8 3.6 online-softmax.1
  485.4 0.0 copy-done.4
  485.4 0.0 copy-start.2
  485.4 2.8 bitcast_add_fusion.1
  488.2 0.0 copy-done.2
  488.2 2.1 fusion.3
  490.3 0.0 all-reduce.15.cloned.1.call-update
  490.3 0.2 all-reduce.17.cloned.1.call-start
  490.5 151.1 %all-reduce.15.cloned.1.call-done = f32[512,512]{1,0:T(8,128)} async-done(((f32[512,512]{1,0:T(8,128)}), f32[512,512]{1,0:T(8,128)}) %all-reduce.15.cloned.1.call-update) | async-done | bytes 1048592 | tf_op jit(solution)/shard_map/psum | solution.py:44
  641.6 0.0 all-reduce.17.cloned.1.call-update
  641.6 64.8 %all-reduce.17.cloned.1.call-done = f32[512,512]{1,0:T(8,128)} async-done(((f32[512,512]{1,0:T(8,128)}), f32[512,512]{1,0:T(8,128)}) %all-reduce.17.cloned.1.call-update) | async-done | bytes 1048592 | tf_op jit(solution)/shard_map/psum | solution.py:44
  706.4 2.3 subtract_multiply_fusion
  708.8 3.6 online-softmax.2
  712.4 2.7 bitcast_add_fusion
  (1 shorter events, 0.0 us)
Async XLA Ops:
  6.5 30.2 %copy-start.3 = (f32[512,256]{1,0:T(8,128)S(1)}, f32[512,256]{1,0:T(8,128)}, u32[]{:S(2)}) copy-start(f32[512,256]{1,0:T(8,128)} %param.5) | copy-start | bytes 1572868
  6.5 178.2 %all-reduce.7.cloned.1.call-start = ((), (), s32[]{:S(2)}) async-start(), calls=%async_computation.1 | async-start | bytes 2097152 | tf_op jit(solution)/shard_map/psum | solution.py:44
  36.7 148.1 %copy-start = (f32[16,32,256]{2,0,1:T(8,128)}, f32[16,32,256]{2,0,1:T(8,128)S(1)}, u32[]{:S(2)}) copy-start(f32[16,32,256]{2,0,1:T(8,128)S(1)} %all_to_all.19) | copy-start | bytes 1572868
  38.8 219.2 %all-reduce.9.cloned.1.call-start = ((), (), s32[]{:S(2)}) async-start(), calls=%async_computation.2 | async-start | bytes 2097152 | tf_op jit(solution)/shard_map/psum | solution.py:44
  184.7 229.9 %all-reduce.11.cloned.1.call-start = ((), (), s32[]{:S(2)}) async-start(), calls=%async_computation.3 | async-start | bytes 2097152 | tf_op jit(solution)/shard_map/psum | solution.py:44
  258.0 6.1 copy-start.6
  260.3 3.7 copy-start.1
  260.3 3.7 copy-start.5
  268.0 211.5 %all-reduce.13.cloned.1.call-start = ((), (), s32[]{:S(2)}) async-start(), calls=%async_computation.4 | async-start | bytes 2097152 | tf_op jit(solution)/shard_map/psum | solution.py:44
  414.7 227.0 %all-reduce.15.cloned.1.call-start = ((), (), s32[]{:S(2)}) async-start(), calls=%async_computation.5 | async-start | bytes 2097152 | tf_op jit(solution)/shard_map/psum | solution.py:44
  481.8 3.6 copy-start.4
  485.4 2.8 copy-start.2
  490.3 216.1 %all-reduce.17.cloned.1.call-start = ((), (), s32[]{:S(2)}) async-start(), calls=%async_computation.6 | async-start | bytes 2097152 | tf_op jit(solution)/shard_map/psum | solution.py:44
Sparse Core Ops, SparseCore 0:
  38.9 145.7 all-reduce.6
  187.1 62.5 all-reduce.8
  268.1 146.4 all-reduce.10
  416.8 62.5 all-reduce.12
  490.4 151.1 all-reduce.14
  643.8 62.5 all-reduce.16
